TPU v7x, 32 devices: a whole 2x2x4 slice. The times are simulated.
32 devices in a mesh: row: 4 (over y, x), col: 8 (over z, core).
Axes of the slice: x: 2, y: 2, z: 4, core: 2. Of those that a mesh axis runs over, the one named last changes fastest.
Arguments:
- pixels_tokens: bfloat16 [4, 2304, 5120], P(None, 'col', 'row'), may hold values from -12 to 12, as said below
- ln_gain: float32 [5120], replicated, may hold values from 0.1 to 1.9
- ln_bias: float32 [5120], replicated, may hold values from -3 to 3
- w_qkv: bfloat16 [5120, 6144], P('col', 'row'), may hold values from -1 to 1, as said below
- w_out: bfloat16 [2048, 5120], P('col', 'row'), may hold values from -0.125 to 0.125
Outputs:
- block_out: bfloat16 [4, 2304, 5120], P(None, 'col', 'row')
Inputs may be any that keep to these rules, and one draw needn't show every extreme that they name: `pixels_tokens`: activations of order one. `w_qkv`: projection entries scaled by the width.
All inputs are finite; a program needn't handle non-finite values.
Results may differ from a plain program's by a relative error of at most 0.012.
The roundings to bfloat16 on the way count: a program that leaves them out, or rounds other values in their place, can miss the bound.
Values may be sent and summed in bfloat16 or wider, within the bound.
No kernel may reach another device: no remote copies, remote signals or barrier semaphores. Data moves between devices by JAX's collectives and lax.ppermute only.
A program may use at most 128 MiB of HBM per device.

v0:
```python
import jax
import jax.numpy as jnp
from jax import lax
from jax.sharding import PartitionSpec as P

HDIM = 128


def layer_norm(values, ln_gain, ln_bias):
    floats = values.astype(jnp.float32)
    center = jnp.mean(floats, axis=-1, keepdims=True)
    spread = jnp.mean((floats - center) * (floats - center), axis=-1, keepdims=True)
    return ((floats - center) * lax.rsqrt(spread + 1e-06) * ln_gain + ln_bias).astype(jnp.bfloat16)


def attend_item(item):
    width = item.shape[1] // 3
    query = item[:, :width]
    keys = item[:, width : 2 * width]
    values = item[:, 2 * width :]
    blocks = query.reshape(4, item.shape[0] // 4, width)

    def one_block(rows):
        scores = jnp.einsum(
            "qd,kd->qk", rows, keys, preferred_element_type=jnp.float32
        ) * width ** (-0.5)
        peak = jnp.max(scores, axis=-1, keepdims=True)
        expo = jnp.exp(scores - peak)
        weights = (expo / jnp.sum(expo, axis=-1, keepdims=True)).astype(jnp.bfloat16)
        return jnp.dot(weights, values, preferred_element_type=jnp.float32).astype(jnp.bfloat16)

    return lax.map(one_block, blocks).reshape(item.shape[0], width)


def local(pixels_tokens, ln_gain, ln_bias, w_qkv, w_out):
    images, seq_col, width_row = pixels_tokens.shape
    col_count = lax.axis_size("col")
    per_head = 3 * HDIM
    head_row = w_qkv.shape[1] // per_head
    items = images * head_row // col_count
    whole = lax.all_gather(pixels_tokens, "row", axis=2, tiled=True)
    normed = layer_norm(whole, ln_gain, ln_bias).reshape(images * seq_col, whole.shape[2])
    columns = normed
    qkv = jnp.dot(
        columns,
        lax.all_gather(w_qkv, "col", axis=0, tiled=True),
        preferred_element_type=jnp.float32,
    ).astype(jnp.bfloat16)
    outgoing = qkv.reshape(images, seq_col, head_row, per_head).transpose(0, 2, 1, 3)
    outgoing = outgoing.reshape(col_count, items, seq_col, per_head).transpose(1, 0, 2, 3)
    received = lax.all_to_all(outgoing, "col", split_axis=1, concat_axis=2, tiled=True)
    count = received.shape[0]
    heads_out = lax.map(attend_item, received.reshape(count, -1, per_head))
    back_send = heads_out.reshape(items, col_count, seq_col, HDIM)
    returned = lax.all_to_all(back_send, "col", split_axis=1, concat_axis=0, tiled=True)
    mixed = (
        returned.reshape(images, head_row, seq_col, HDIM)
        .transpose(0, 2, 1, 3)
        .reshape(images, seq_col, head_row * HDIM)
    )
    gathered = lax.all_gather(mixed, "row", axis=2, tiled=True)
    flat_heads = gathered.reshape(images * seq_col, gathered.shape[2])
    columns = flat_heads
    projected = jnp.dot(
        columns,
        lax.all_gather(w_out, "col", axis=0, tiled=True),
        preferred_element_type=jnp.float32,
    )
    summed = pixels_tokens.astype(jnp.float32) + projected.reshape(images, seq_col, width_row)
    return summed.astype(jnp.bfloat16)


def solution(mesh):
    in_specs = (P(None, "col", "row"), P(), P(), P("col", "row"), P("col", "row"))
    out_specs = P(None, "col", "row")
    return jax.shard_map(local, mesh=mesh, in_specs=in_specs, out_specs=out_specs, check_vma=False)
```

profile of v0, /device:TPU:0, one launch (start us, length us, event | category | flops | bytes accessed | tf_op | source)
XLA Modules:
  0.0 570.9 jit_solution(7235709859060408799)
XLA Ops:
  6.5 0.7 all-gather.5.cloned.1.call-update
  7.3 0.0 all-gather.7.cloned.1.call-start
  7.3 0.7 all-gather.7.cloned.1.call-update
  8.0 119.8 %all-gather.5.cloned.1.call-done = bf16[4,288,5120]{2,1,0:T(8,128)(2,1)} async-done(((bf16[4,288,1280]{2,1,0:T(8,128)(2,1)}), bf16[4,288,5120]{2,1,0:T(8,128)(2,1)}) %all-gather.5.cloned.1.call-update) | async-done | bytes 11796496 | tf_op jit(solution)/shard_map/all_gather | solution.py:41
  127.8 6.0 %convert_reduce_fusion = f32[4,288]{1,0:T(4,128)S(1)} fusion(bf16[4,288,5120]{2,1,0:T(8,128)(2,1)} %all-gather.5.cloned.1.call-done), kind=kLoop, calls=%fused_computation.14 | loop fusion | flops 11795328 | bytes 11801088 | tf_op jit(solution)/shard_map/reduce_sum | solution.py:11
  133.8 0.0 copy-start.4
  133.8 8.6 %fusion.10 = f32[4,288]{1,0:T(4,128)S(1)} fusion(bf16[4,288,5120]{2,1,0:T(8,128)(2,1)} %all-gather.5.cloned.1.call-done, f32[4,288]{1,0:T(4,128)S(1)} %broadcast_multiply_fusion), kind=kLoop, calls=%fused_computation.17 | loop fusion | flops 23591808 | bytes 11805696 | tf_op jit(solution)/shard_map/reduce_sum | solution.py:12
  142.5 12.3 %fusion.13 = bf16[4,288,5120]{2,1,0:T(8,128)(2,1)} fusion(bf16[4,288,5120]{2,1,0:T(8,128)(2,1)} %all-gather.5.cloned.1.call-done, f32[5120]{0:T(1024)S(1)} %copy-done.3, f32[5120]{0:T(1024)S(1)} %copy-done.4, f32[4,288]{1,0:T(4,128)S(1)} %add_rsqrt_fusion, f32[4,288]{1,0:T(4,128)S(1)} %broadcast_multiply_fusion), kind=kLoop, calls=%fused_computation.20 | loop fusion | flops 35389440 | bytes 23643136 | tf_op jit(solution)/shard_map/convert_element_type | solution.py:13
  154.8 117.2 %all-gather.7.cloned.1.call-done = bf16[5120,1536]{1,0:T(8,128)(2,1)} async-done(((bf16[640,1536]{1,0:T(8,128)(2,1)}), bf16[5120,1536]{1,0:T(8,128)(2,1)}) %all-gather.7.cloned.1.call-update) | async-done | bytes 15728656 | tf_op jit(solution)/shard_map/all_gather | solution.py:46
  271.9 25.9 %convolution_convert_fusion = bf16[1152,1536]{1,0:T(8,128)(2,1)} fusion(bf16[1152,5120]{1,0:T(8,128)(2,1)} %bitcast.61, bf16[5120,1536]{1,0:T(8,128)(2,1)} %all-gather.7.cloned.1.call-done), kind=kOutput, calls=%fused_computation.21 | convolution fusion | flops 18121162752 | bytes 31064064 | tf_op jit(solution)/shard_map/dot_general | solution.py:44
  297.9 5.8 %reshape.52 = bf16[4,288,4,384]{3,2,1,0:T(4,128)(2,1)S(1)} reshape(bf16[1152,1536]{1,0:T(8,128)(2,1)} %convolution_convert_fusion) | data formatting | bytes 7077888 | tf_op jit(solution)/shard_map/reshape | solution.py:49
  303.7 2.3 copy.12
  306.0 3.7 all-to-all-start
  309.7 0.0 all-gather.11.cloned.1.call-start
  309.7 0.7 all-gather.11.cloned.1.call-update
  310.4 0.2 all-gather.9.cloned.1.call-start
  310.6 121.0 %all-to-all-done = bf16[2,8,288,384]{3,2,0,1:T(8,128)(2,1)S(1)} async-done(((bf16[2,8,288,384]{3,2,0,1:T(8,128)(2,1)}), bf16[2,8,288,384]{3,2,0,1:T(8,128)(2,1)S(1)}, u32[]{:S(2)}, u32[]{:S(2)}) %all-to-all-start) | async-done | bytes 3538976 | tf_op jit(solution)/shard_map/all_to_all | solution.py:51
  431.7 2.2 copy.13
  433.8 29.4 %while.21 = (s32[]{:T(128)}, bf16[2,2304,128]{2,1,0:T(8,128)(2,1)}, bf16[2,2304,384]{2,1,0:T(8,128)(2,1)}, s32[]{:T(128)}, s32[]{:T(128)}, /*index=5*/s32[]{:T(128)}) while((s32[]{:T(128)}, bf16[2,2304,128]{2,1,0:T(8,128)(2,1)}, bf16[2,2304,384]{2,1,0:T(8,128)(2,1)}, s32[]{:T(128)}, s32[]{:T(128)}, /*index=5*/s32[]{:T(128)}) %tuple.44), condition=%wide.region_7.8_spmd, body=%wide.region_2.7_spmd.sunk | while | flops 688839552 | bytes 35109896 | solution.py:53
  433.8 1.7 dynamic-slice_bitcast_fusion.2
  435.5 0.3 fusion.31
  435.8 0.0 copy-start.1
  435.8 11.6 %while.22 = (s32[]{:T(128)}, bf16[4,576,128]{2,1,0:T(8,128)(2,1)S(1)}, bf16[4,576,128]{2,1,0:T(8,128)(2,1)S(1)}, bf16[2304,128]{1,0:T(8,128)(2,1)S(1)}, bf16[2304,128]{1,0:T(8,128)(2,1)S(1)}, /*index=5*/s32[]{:T(128)}) while((s32[]{:T(128)}, bf16[4,576,128]{2,1,0:T(8,128)(2,1)S(1)}, bf16[4,576,128]{2,1,0:T(8,128)(2,1)S(1)}, ...), condition=%wide.region_6.6_spmd, body=%wide.region_3.5_spmd.sunk | while | flops 688839552 | bytes 17414988 | solution.py:32
  435.8 0.9 fusion.34
  436.8 0.9 fusion.35
  437.7 1.1 fusion.36
  438.7 0.9 fusion.34
  439.7 0.9 fusion.35
  440.6 1.1 fusion.36
  441.6 0.9 fusion.34
  442.6 0.9 fusion.35
  443.5 1.1 fusion.36
  444.5 0.9 fusion.34
  445.5 0.9 fusion.35
  446.4 1.1 fusion.36
  447.4 0.1 bitcast_dynamic-update-slice_fusion.2
  447.5 0.0 copy-start.2
  447.5 1.0 copy-done.2
  448.5 1.7 dynamic-slice_bitcast_fusion.2
  450.2 0.3 fusion.31
  450.5 0.0 copy-start.1
  450.5 11.6 %while.22 = (s32[]{:T(128)}, bf16[4,576,128]{2,1,0:T(8,128)(2,1)S(1)}, bf16[4,576,128]{2,1,0:T(8,128)(2,1)S(1)}, bf16[2304,128]{1,0:T(8,128)(2,1)S(1)}, bf16[2304,128]{1,0:T(8,128)(2,1)S(1)}, /*index=5*/s32[]{:T(128)}) while((s32[]{:T(128)}, bf16[4,576,128]{2,1,0:T(8,128)(2,1)S(1)}, bf16[4,576,128]{2,1,0:T(8,128)(2,1)S(1)}, ...), condition=%wide.region_6.6_spmd, body=%wide.region_3.5_spmd.sunk | while | flops 688839552 | bytes 17414988 | solution.py:32
  450.5 0.9 fusion.34
  451.5 0.9 fusion.35
  452.4 1.1 fusion.36
  453.4 0.9 fusion.34
  454.4 0.9 fusion.35
  455.3 1.1 fusion.36
  456.3 0.9 fusion.34
  457.3 0.9 fusion.35
  458.2 1.1 fusion.36
  459.2 0.9 fusion.34
  460.2 0.9 fusion.35
  461.1 1.1 fusion.36
  462.1 0.1 bitcast_dynamic-update-slice_fusion.2
  462.2 0.0 copy-start.2
  462.2 1.0 copy-done.2
  463.2 1.5 copy.14
  464.8 31.8 %all_to_all.24 = bf16[2,8,288,128]{3,2,0,1:T(8,128)(2,1)S(1)} all-to-all(bf16[2,8,288,128]{3,2,0,1:T(8,128)(2,1)S(1)} %copy.14), channel_id=1, replica_groups=mesh['row'=4,'col'=8] {'col'}, dimensions={1} | all-to-all | bytes 2359296 | tf_op jit(solution)/shard_map/all_to_all | solution.py:55
  496.5 1.2 copy.18
  497.8 0.0 all-gather.9.cloned.1.call-update
  497.8 0.0 all-gather.11.cloned.1.call-done
  497.8 55.8 %all-gather.9.cloned.1.call-done = bf16[4,288,2048]{2,1,0:T(8,128)(2,1)} async-done(((bf16[4,288,512]{2,1,0:T(8,128)(2,1)}), bf16[4,288,2048]{2,1,0:T(8,128)(2,1)}) %all-gather.9.cloned.1.call-update) | async-done | bytes 4718608 | tf_op jit(solution)/shard_map/all_gather | solution.py:61
  553.6 10.8 %add_convert_fusion = bf16[4,288,1280]{2,1,0:T(8,128)(2,1)} fusion(bf16[4,288,1280]{2,1,0:T(8,128)(2,1)S(1)} %copy-done, bf16[4,288,2048]{2,1,0:T(8,128)(2,1)} %all-gather.9.cloned.1.call-done, bf16[2048,1280]{1,0:T(8,128)(2,1)} %all-gather.11.cloned.1.call-done), kind=kOutput, calls=%fused_computation.22 | convolution fusion | flops 6044221440 | bytes 15859712 | tf_op jit(solution)/shard_map/dot_general | solution.py:64
  (13 shorter events, 0.0 us)
Async XLA Ops:
  6.5 121.2 %all-gather.5.cloned.1.call-start = ((), (), s32[]{:S(2)}) async-start(), calls=%async_computation.2 | async-start | bytes 14745600 | tf_op jit(solution)/shard_map/all_gather | solution.py:41
  7.3 264.7 %all-gather.7.cloned.1.call-start = ((), (), s32[]{:S(2)}) async-start(), calls=%async_computation.3 | async-start | bytes 17694720 | tf_op jit(solution)/shard_map/all_gather | solution.py:46
  133.8 8.7 %copy-start.3 = (f32[5120]{0:T(1024)S(1)}, f32[5120]{0:T(1024)}, u32[]{:S(2)}) copy-start(f32[5120]{0:T(1024)} %param.11) | copy-start | bytes 61444
  133.8 8.7 %copy-start.4 = (f32[5120]{0:T(1024)S(1)}, f32[5120]{0:T(1024)}, u32[]{:S(2)}) copy-start(f32[5120]{0:T(1024)} %param.10) | copy-start | bytes 61444
  306.0 125.7 %all-to-all-start = ((bf16[2,8,288,384]{3,2,0,1:T(8,128)(2,1)}), bf16[2,8,288,384]{3,2,0,1:T(8,128)(2,1)S(1)}, u32[]{:S(2)}, u32[]{:S(2)}) async-start(bf16[2,8,288,384]{3,2,0,1:T(8,128)(2,1)} %bitcast.60), calls=%async_computation | async-start | bytes 7077888 | tf_op jit(solution)/shard_map/all_to_all | solution.py:51
  309.7 188.1 %all-gather.11.cloned.1.call-start = ((), (), s32[]{:S(2)}) async-start(), calls=%async_computation.5 | async-start | bytes 5898240 | tf_op jit(solution)/shard_map/all_gather | solution.py:66
  310.4 243.2 %all-gather.9.cloned.1.call-start = ((), (), s32[]{:S(2)}) async-start(), calls=%async_computation.4 | async-start | bytes 5898240 | tf_op jit(solution)/shard_map/all_gather | solution.py:61
  435.8 11.6 %copy-start.1 = (bf16[2,2304,128]{2,1,0:T(8,128)(2,1)S(1)}, bf16[2,2304,128]{2,1,0:T(8,128)(2,1)}, u32[]{:S(2)}) copy-start(bf16[2,2304,128]{2,1,0:T(8,128)(2,1)} %get-tuple-element.169) | copy-start | bytes 3538948 | tf_op jit(solution)/shard_map/while
  447.5 1.0 copy-start.2
  450.5 11.6 %copy-start.1 = (bf16[2,2304,128]{2,1,0:T(8,128)(2,1)S(1)}, bf16[2,2304,128]{2,1,0:T(8,128)(2,1)}, u32[]{:S(2)}) copy-start(bf16[2,2304,128]{2,1,0:T(8,128)(2,1)} %get-tuple-element.169) | copy-start | bytes 3538948 | tf_op jit(solution)/shard_map/while
  462.2 1.0 copy-start.2
  463.2 90.3 %copy-start = (bf16[4,288,1280]{2,1,0:T(8,128)(2,1)S(1)}, bf16[4,288,1280]{2,1,0:T(8,128)(2,1)}, u32[]{:S(2)}) copy-start(bf16[4,288,1280]{2,1,0:T(8,128)(2,1)} %param.9) | copy-start | bytes 8847364
Sparse Core Ops, SparseCore 0:
  9.2 118.5 all-gather.4
  129.4 142.4 all-gather.6
  312.1 110.7 all-gather.10
  497.9 55.6 all-gather.8
where the time goes:
time: 571 us
  waiting for transfers between devices  416 us (73%)
  matrix products  52.8 us (9%)
  other arithmetic  33.9 us (6%)
  blocking collectives  31.8 us (6%)
  local copies, waits for them, and re-layouts  19.1 us (3%)
  between operations  13.2 us (2%)
    all_to_all x1, waiting for transfers between devices, local(): lax.all_to_all(outgoing, 'col', split_axis=1, concat_axis=2, tiled=True)  121 us
    all_gather x1, waiting for transfers between devices, local(): whole = lax.all_gather(pixels_tokens, 'row', axis=2, tiled=True)  120 us
    all_gather x1, waiting for transfers between devices, local(): lax.all_gather(w_qkv, 'col', axis=0, tiled=True)  117 us
    all_gather x1, waiting for transfers between devices, local(): gathered = lax.all_gather(mixed, 'row', axis=2, tiled=True)  55.8 us
    all_to_all x1, blocking collectives, local(): lax.all_to_all(back_send, 'col', split_axis=1, concat_axis=0, tiled=True)  31.8 us
    dot_general x1, matrix products, local(): jnp.dot(columns, lax.all_gather(w_qkv, 'col', axis=0, tiled=True), prefer...  25.9 us
    convert_element_type x1, other arithmetic, layer_norm(): ((floats - center) * lax.rsqrt(spread + 1e-06) * ln_gain + ln_bias).astyp...  12.3 us
  transfers between devices with their start and end apart: 5, of which 4 were waited for; matrix products, arithmetic and copies ran while one was open for 10% of the time, Pallas kernels for 0%

commit v1 on v0

--- a/solution.py
+++ b/solution.py
@@ -48,7 +48,9 @@
     ).astype(jnp.bfloat16)
     outgoing = qkv.reshape(images, seq_col, head_row, per_head).transpose(0, 2, 1, 3)
     outgoing = outgoing.reshape(col_count, items, seq_col, per_head).transpose(1, 0, 2, 3)
-    received = lax.all_to_all(outgoing, "col", split_axis=1, concat_axis=2, tiled=True)
+    parts = jnp.split(outgoing, lax.axis_size("col"), axis=1)
+    incoming = lax.all_to_all(jnp.stack(parts), "col", 0, 0)
+    received = jnp.concatenate(incoming, axis=2)
     count = received.shape[0]
     heads_out = lax.map(attend_item, received.reshape(count, -1, per_head))
     back_send = heads_out.reshape(items, col_count, seq_col, HDIM)

time: 571 us -> 576 us (level)
  no operation moved by 1% of the time
where the time goes in v1:
time: 576 us
  waiting for transfers between devices  416 us (72%)
  matrix products  52.8 us (9%)
  other arithmetic  33.9 us (6%)
  blocking collectives  32 us (6%)
  local copies, waits for them, and re-layouts  23.7 us (4%)
  between operations  13.2 us (2%)
    all_to_all x1, waiting for transfers between devices, local(): incoming = lax.all_to_all(jnp.stack(parts), 'col', 0, 0)  121 us
    all_gather x1, waiting for transfers between devices, local(): whole = lax.all_gather(pixels_tokens, 'row', axis=2, tiled=True)  120 us
    all_gather x1, waiting for transfers between devices, local(): lax.all_gather(w_qkv, 'col', axis=0, tiled=True)  117 us
    all_gather x1, waiting for transfers between devices, local(): gathered = lax.all_gather(mixed, 'row', axis=2, tiled=True)  55.7 us
    all_to_all x1, blocking collectives, local(): lax.all_to_all(back_send, 'col', split_axis=1, concat_axis=0, tiled=True)  32 us
    dot_general x1, matrix products, local(): jnp.dot(columns, lax.all_gather(w_qkv, 'col', axis=0, tiled=True), prefer...  25.9 us
    convert_element_type x1, other arithmetic, layer_norm(): ((floats - center) * lax.rsqrt(spread + 1e-06) * ln_gain + ln_bias).astyp...  12.3 us
  transfers between devices with their start and end apart: 5, of which 4 were waited for; matrix products, arithmetic and copies ran while one was open for 10% of the time, Pallas kernels for 0%

profile of v1, /device:TPU:0, one launch (start us, length us, event | category | flops | bytes accessed | tf_op | source)
XLA Modules:
  0.0 575.8 jit_solution(10762015638492208365)
XLA Ops:
  6.5 0.7 all-gather.5.cloned.1.call-update
  7.3 0.7 all-gather.7.cloned.1.call-update
  8.0 119.8 %all-gather.5.cloned.1.call-done = bf16[4,288,5120]{2,1,0:T(8,128)(2,1)} async-done(((bf16[4,288,1280]{2,1,0:T(8,128)(2,1)}), bf16[4,288,5120]{2,1,0:T(8,128)(2,1)}) %all-gather.5.cloned.1.call-update) | async-done | bytes 11796496 | tf_op jit(solution)/shard_map/all_gather | solution.py:41
  127.8 6.0 %convert_reduce_fusion = f32[4,288]{1,0:T(4,128)S(1)} fusion(bf16[4,288,5120]{2,1,0:T(8,128)(2,1)} %all-gather.5.cloned.1.call-done), kind=kLoop, calls=%fused_computation.14 | loop fusion | flops 11795328 | bytes 11801088 | tf_op jit(solution)/shard_map/reduce_sum | solution.py:11
  133.8 8.6 %fusion.10 = f32[4,288]{1,0:T(4,128)S(1)} fusion(bf16[4,288,5120]{2,1,0:T(8,128)(2,1)} %all-gather.5.cloned.1.call-done, f32[4,288]{1,0:T(4,128)S(1)} %broadcast_multiply_fusion), kind=kLoop, calls=%fused_computation.17 | loop fusion | flops 23591808 | bytes 11805696 | tf_op jit(solution)/shard_map/reduce_sum | solution.py:12
  142.5 12.3 %fusion.13 = bf16[4,288,5120]{2,1,0:T(8,128)(2,1)} fusion(bf16[4,288,5120]{2,1,0:T(8,128)(2,1)} %all-gather.5.cloned.1.call-done, f32[5120]{0:T(1024)S(1)} %copy-done.3, f32[5120]{0:T(1024)S(1)} %copy-done.4, f32[4,288]{1,0:T(4,128)S(1)} %add_rsqrt_fusion, f32[4,288]{1,0:T(4,128)S(1)} %broadcast_multiply_fusion), kind=kLoop, calls=%fused_computation.20 | loop fusion | flops 35389440 | bytes 23643136 | tf_op jit(solution)/shard_map/convert_element_type | solution.py:13
  154.8 117.2 %all-gather.7.cloned.1.call-done = bf16[5120,1536]{1,0:T(8,128)(2,1)} async-done(((bf16[640,1536]{1,0:T(8,128)(2,1)}), bf16[5120,1536]{1,0:T(8,128)(2,1)}) %all-gather.7.cloned.1.call-update) | async-done | bytes 15728656 | tf_op jit(solution)/shard_map/all_gather | solution.py:46
  271.9 25.9 %convolution_convert_fusion = bf16[1152,1536]{1,0:T(8,128)(2,1)} fusion(bf16[1152,5120]{1,0:T(8,128)(2,1)} %bitcast.102, bf16[5120,1536]{1,0:T(8,128)(2,1)} %all-gather.7.cloned.1.call-done), kind=kOutput, calls=%fused_computation.21 | convolution fusion | flops 18121162752 | bytes 31064064 | tf_op jit(solution)/shard_map/dot_general | solution.py:44
  297.9 5.8 %reshape.48 = bf16[4,288,4,384]{3,2,1,0:T(4,128)(2,1)S(1)} reshape(bf16[1152,1536]{1,0:T(8,128)(2,1)} %convolution_convert_fusion) | data formatting | bytes 7077888 | tf_op jit(solution)/shard_map/reshape | solution.py:49
  303.7 0.5 copy.19
  304.2 0.8 fusion.25
  305.0 0.8 fusion.24
  305.8 0.8 fusion.23
  306.6 0.8 fusion.22
  307.4 0.8 fusion.21
  308.2 0.8 fusion.20
  309.1 0.9 fusion.19
  309.9 0.8 fusion.18
  310.7 3.7 all-to-all-start
  314.4 0.0 all-gather.11.cloned.1.call-start
  314.5 0.7 all-gather.11.cloned.1.call-update
  315.2 0.2 all-gather.9.cloned.1.call-start
  315.4 121.0 %all-to-all-done = bf16[8,2,1,288,384]{4,3,1,2,0:T(8,128)(2,1)S(1)} async-done(((bf16[8,2,1,288,384]{4,3,1,2,0:T(8,128)(2,1)}), bf16[8,2,1,288,384]{4,3,1,2,0:T(8,128)(2,1)S(1)}, u32[]{:S(2)}, u32[]{:S(2)}) %all-to-all-start) | async-done | bytes 3538976 | tf_op jit(solution)/shard_map/all_to_all | solution.py:52
  436.4 2.2 copy.20
  438.6 29.4 %while.21 = (s32[]{:T(128)}, bf16[2,2304,128]{2,1,0:T(8,128)(2,1)}, bf16[2,2304,384]{2,1,0:T(8,128)(2,1)}, s32[]{:T(128)}, s32[]{:T(128)}, /*index=5*/s32[]{:T(128)}) while((s32[]{:T(128)}, bf16[2,2304,128]{2,1,0:T(8,128)(2,1)}, bf16[2,2304,384]{2,1,0:T(8,128)(2,1)}, s32[]{:T(128)}, s32[]{:T(128)}, /*index=5*/s32[]{:T(128)}) %tuple.44), condition=%wide.region_7.8_spmd, body=%wide.region_2.7_spmd.sunk | while | flops 688839552 | bytes 35109896 | solution.py:55
  438.6 1.7 dynamic-slice_bitcast_fusion.2
  440.3 0.3 fusion.39
  440.6 11.6 %while.22 = (s32[]{:T(128)}, bf16[4,576,128]{2,1,0:T(8,128)(2,1)S(1)}, bf16[4,576,128]{2,1,0:T(8,128)(2,1)S(1)}, bf16[2304,128]{1,0:T(8,128)(2,1)S(1)}, bf16[2304,128]{1,0:T(8,128)(2,1)S(1)}, /*index=5*/s32[]{:T(128)}) while((s32[]{:T(128)}, bf16[4,576,128]{2,1,0:T(8,128)(2,1)S(1)}, bf16[4,576,128]{2,1,0:T(8,128)(2,1)S(1)}, ...), condition=%wide.region_6.6_spmd, body=%wide.region_3.5_spmd.sunk | while | flops 688839552 | bytes 17414988 | solution.py:32
  440.6 0.9 fusion.42
  441.6 0.9 fusion.43
  442.4 1.1 fusion.44
  443.5 1.0 fusion.42
  444.5 0.9 fusion.43
  445.3 1.1 fusion.44
  446.4 1.0 fusion.42
  447.4 0.9 fusion.43
  448.2 1.1 fusion.44
  449.3 1.0 fusion.42
  450.3 0.9 fusion.43
  451.1 1.1 fusion.44
  452.2 0.1 bitcast_dynamic-update-slice_fusion.2
  452.3 1.0 copy-done.2
  453.3 1.7 dynamic-slice_bitcast_fusion.2
  455.0 0.3 fusion.39
  455.3 11.6 %while.22 = (s32[]{:T(128)}, bf16[4,576,128]{2,1,0:T(8,128)(2,1)S(1)}, bf16[4,576,128]{2,1,0:T(8,128)(2,1)S(1)}, bf16[2304,128]{1,0:T(8,128)(2,1)S(1)}, bf16[2304,128]{1,0:T(8,128)(2,1)S(1)}, /*index=5*/s32[]{:T(128)}) while((s32[]{:T(128)}, bf16[4,576,128]{2,1,0:T(8,128)(2,1)S(1)}, bf16[4,576,128]{2,1,0:T(8,128)(2,1)S(1)}, ...), condition=%wide.region_6.6_spmd, body=%wide.region_3.5_spmd.sunk | while | flops 688839552 | bytes 17414988 | solution.py:32
  455.3 1.0 fusion.42
  456.3 0.9 fusion.43
  457.2 1.1 fusion.44
  458.2 0.9 fusion.42
  459.2 0.9 fusion.43
  460.0 1.1 fusion.44
  461.1 0.9 fusion.42
  462.1 0.9 fusion.43
  462.9 1.1 fusion.44
  464.0 0.9 fusion.42
  465.0 0.9 fusion.43
  465.8 1.1 fusion.44
  466.9 0.1 bitcast_dynamic-update-slice_fusion.2
  467.0 1.0 copy-done.2
  468.0 1.3 copy.21
  469.4 32.0 %all_to_all.20 = bf16[2,8,288,128]{3,2,0,1:T(8,128)(2,1)S(1)} all-to-all(bf16[2,8,288,128]{3,2,0,1:T(8,128)(2,1)S(1)} %copy.21), channel_id=1, replica_groups=mesh['row'=4,'col'=8] {'col'}, dimensions={1} | all-to-all | bytes 2359296 | tf_op jit(solution)/shard_map/all_to_all | solution.py:57
  501.4 1.2 copy.25
  502.7 55.7 %all-gather.9.cloned.1.call-done = bf16[4,288,2048]{2,1,0:T(8,128)(2,1)} async-done(((bf16[4,288,512]{2,1,0:T(8,128)(2,1)}), bf16[4,288,2048]{2,1,0:T(8,128)(2,1)}) %all-gather.9.cloned.1.call-update) | async-done | bytes 4718608 | tf_op jit(solution)/shard_map/all_gather | solution.py:63
  558.5 10.8 %add_convert_fusion = bf16[4,288,1280]{2,1,0:T(8,128)(2,1)} fusion(bf16[4,288,1280]{2,1,0:T(8,128)(2,1)S(1)} %copy-done, bf16[4,288,2048]{2,1,0:T(8,128)(2,1)} %all-gather.9.cloned.1.call-done, bf16[2048,1280]{1,0:T(8,128)(2,1)} %all-gather.11.cloned.1.call-done), kind=kOutput, calls=%fused_computation.22 | convolution fusion | flops 6044221440 | bytes 15859712 | tf_op jit(solution)/shard_map/dot_general | solution.py:66
  (21 shorter events, 0.1 us)
Async XLA Ops:
  6.5 121.2 %all-gather.5.cloned.1.call-start = ((), (), s32[]{:S(2)}) async-start(), calls=%async_computation.2 | async-start | bytes 14745600 | tf_op jit(solution)/shard_map/all_gather | solution.py:41
  7.3 264.7 %all-gather.7.cloned.1.call-start = ((), (), s32[]{:S(2)}) async-start(), calls=%async_computation.3 | async-start | bytes 17694720 | tf_op jit(solution)/shard_map/all_gather | solution.py:46
  133.8 8.7 %copy-start.3 = (f32[5120]{0:T(1024)S(1)}, f32[5120]{0:T(1024)}, u32[]{:S(2)}) copy-start(f32[5120]{0:T(1024)} %param.11) | copy-start | bytes 61444
  133.8 8.7 %copy-start.4 = (f32[5120]{0:T(1024)S(1)}, f32[5120]{0:T(1024)}, u32[]{:S(2)}) copy-start(f32[5120]{0:T(1024)} %param.10) | copy-start | bytes 61444
  310.7 125.7 %all-to-all-start = ((bf16[8,2,1,288,384]{4,3,1,2,0:T(8,128)(2,1)}), bf16[8,2,1,288,384]{4,3,1,2,0:T(8,128)(2,1)S(1)}, u32[]{:S(2)}, u32[]{:S(2)}) async-start(bf16[8,2,1,288,384]{4,3,1,2,0:T(8,128)(2,1)} %fusion.18), calls=%async_computation | async-start | bytes 7077888 | tf_op jit(solution)/shard_map/all_to_all | solution.py:52
  314.4 188.3 %all-gather.11.cloned.1.call-start = ((), (), s32[]{:S(2)}) async-start(), calls=%async_computation.5 | async-start | bytes 5898240 | tf_op jit(solution)/shard_map/all_gather | solution.py:68
  315.2 243.3 %all-gather.9.cloned.1.call-start = ((), (), s32[]{:S(2)}) async-start(), calls=%async_computation.4 | async-start | bytes 5898240 | tf_op jit(solution)/shard_map/all_gather | solution.py:63
  440.6 11.6 %copy-start.1 = (bf16[2,2304,128]{2,1,0:T(8,128)(2,1)S(1)}, bf16[2,2304,128]{2,1,0:T(8,128)(2,1)}, u32[]{:S(2)}) copy-start(bf16[2,2304,128]{2,1,0:T(8,128)(2,1)} %get-tuple-element.169) | copy-start | bytes 3538948 | tf_op jit(solution)/shard_map/while
  452.3 1.0 copy-start.2
  455.3 11.6 %copy-start.1 = (bf16[2,2304,128]{2,1,0:T(8,128)(2,1)S(1)}, bf16[2,2304,128]{2,1,0:T(8,128)(2,1)}, u32[]{:S(2)}) copy-start(bf16[2,2304,128]{2,1,0:T(8,128)(2,1)} %get-tuple-element.169) | copy-start | bytes 3538948 | tf_op jit(solution)/shard_map/while
  467.0 1.0 copy-start.2
  469.4 89.1 %copy-start = (bf16[4,288,1280]{2,1,0:T(8,128)(2,1)S(1)}, bf16[4,288,1280]{2,1,0:T(8,128)(2,1)}, u32[]{:S(2)}) copy-start(bf16[4,288,1280]{2,1,0:T(8,128)(2,1)} %param.9) | copy-start | bytes 8847364
Sparse Core Ops, SparseCore 0:
  9.2 118.5 all-gather.4
  129.4 142.4 all-gather.6
  316.9 110.7 all-gather.10
  502.8 55.6 all-gather.8
